TPU v7x, 128 devices: a whole 4x4x4 slice. The times are simulated.
128 devices in a mesh: row: 8 (over x, z_lo), col: 16 (over z_hi, y, core).
Axes of the slice: x: 4, y: 4, z: 4 (z_hi: 2, z_lo: 2; z = z_hi * 2 + z_lo), core: 2. Of those that a mesh axis runs over, the one named last changes fastest.
Arguments:
- pair: bfloat16 [512, 512, 128], P('row', 'col'), may hold values from -6 to 6
- cotangent: bfloat16 [512, 512, 128], P('row', 'col'), may hold values from -6 to 6
- res_mask: int32 [512], replicated, may hold values 0 or 1
- chain: int32 [512], replicated, may hold values from 0 to 3, never falling along the last dimension, each value on 1 to 256 neighbouring positions
- ln_in_gain: float32 [128], replicated, may hold values from 0.5 to 1.5
- ln_in_bias: float32 [128], replicated, may hold values from -3 to 3
- w_proj: bfloat16 [128, 512], replicated, may hold values from -0.5 to 0.5
- w_gate: bfloat16 [128, 128], replicated, may hold values from -0.5 to 0.5
- chain_bias: float32 [128], replicated, may hold values from -4 to 4
- ln_out_gain: float32 [128], replicated, may hold values from 0.5 to 1.5
- ln_out_bias: float32 [128], replicated, may hold values from -3 to 3
- w_out: bfloat16 [128, 128], replicated, may hold values from -0.5 to 0.5
Outputs:
- grad_pair: bfloat16 [512, 512, 128], P('row', 'col')
- grad_proj: float32 [128, 512], replicated
- grad_gate: float32 [128, 128], replicated
- grad_out: float32 [128, 128], replicated
Inputs may be any that keep to these rules, and one draw needn't show every extreme that they name: chain never decreases along the residues.
All inputs are finite; a program needn't handle non-finite values.
Results may differ from a plain program's by a relative error of at most 0.02.
Values may be sent and summed in bfloat16 or wider, within the bound.
No kernel may reach another device: no remote copies, remote signals or barrier semaphores. Data moves between devices by JAX's collectives and lax.ppermute only.
A program may use at most 128 MiB of HBM per device.

v0:
```python
import jax
import jax.numpy as jnp
from jax import lax
from jax.sharding import PartitionSpec as P

EPS = 1e-05


def layer_norm(values, gain, bias):
    mean = jnp.mean(values, axis=-1, keepdims=True)
    centred = values - mean
    inverse = lax.rsqrt(jnp.mean(centred * centred, axis=-1, keepdims=True) + EPS)
    normed = centred * inverse
    return (normed * gain + bias, normed, inverse)


def norm_back(grad_normed, normed, inverse):
    first = jnp.mean(grad_normed, axis=-1, keepdims=True)
    second = jnp.mean(grad_normed * normed, axis=-1, keepdims=True)
    return (grad_normed - first - normed * second) * inverse


def matmul_last(left, right):
    shape = left.shape
    flat = jnp.dot(left.reshape(-1, shape[-1]), right, preferred_element_type=jnp.float32)
    return flat.reshape(shape[:-1] + (right.shape[1],))


def contract_pairs(left, right):
    flat_left = left.reshape(-1, left.shape[-1])
    flat_right = right.reshape(-1, right.shape[-1])
    return lax.dot_general(
        flat_left, flat_right, (((0,), (0,)), ((), ())), preferred_element_type=jnp.float32
    )


def project(pair, ln_in_gain, ln_in_bias, w_proj):
    scaled, normed, inverse = layer_norm(pair.astype(jnp.float32), ln_in_gain, ln_in_bias)
    normed_b = scaled.astype(jnp.bfloat16)
    return (normed_b, normed, inverse, matmul_last(normed_b, w_proj))


def activations(proj, pair_mask):
    width = proj.shape[-1] // 4
    gate_a = jax.nn.sigmoid(proj[..., :width])
    gate_b = jax.nn.sigmoid(proj[..., 2 * width : 3 * width])
    act_a = (gate_a * proj[..., width : 2 * width] * pair_mask).astype(jnp.bfloat16)
    act_b = (gate_b * proj[..., 3 * width :] * pair_mask).astype(jnp.bfloat16)
    return (act_a, act_b)


def gated_output(
    mixed, cotangent, normed_b, same, chain_bias, w_gate, ln_out_gain, ln_out_bias, w_out
):
    scaled, normed, inverse = layer_norm(mixed, ln_out_gain, ln_out_bias)
    out_b = scaled.astype(jnp.bfloat16)
    update = matmul_last(out_b, w_out)
    gate = jax.nn.sigmoid(matmul_last(normed_b, w_gate) + same * chain_bias)
    cot = cotangent.astype(jnp.float32)
    grad_update = (cot * gate).astype(jnp.bfloat16)
    grad_logit = (cot * update * gate * (1.0 - gate)).astype(jnp.bfloat16)
    grad_scaled = matmul_last(grad_update, w_out.T)
    grad_mixed = norm_back(grad_scaled * ln_out_gain, normed, inverse).astype(jnp.bfloat16)
    return (
        grad_mixed,
        grad_logit,
        contract_pairs(out_b, grad_update),
        contract_pairs(normed_b, grad_logit),
    )


def input_back(
    normed_b,
    normed,
    inverse,
    proj,
    pair_mask,
    grad_a,
    grad_b,
    grad_logit,
    ln_in_gain,
    w_proj,
    w_gate,
):
    width = proj.shape[-1] // 4
    gate_a = jax.nn.sigmoid(proj[..., :width])
    gate_b = jax.nn.sigmoid(proj[..., 2 * width : 3 * width])
    masked_a = grad_a * pair_mask
    masked_b = grad_b * pair_mask
    grad_p = jnp.concatenate(
        [
            masked_a * proj[..., width : 2 * width] * gate_a * (1.0 - gate_a),
            masked_a * gate_a,
            masked_b * proj[..., 3 * width :] * gate_b * (1.0 - gate_b),
            masked_b * gate_b,
        ],
        axis=-1,
    ).astype(jnp.bfloat16)
    grad_zn = matmul_last(grad_p, w_proj.T) + matmul_last(grad_logit, w_gate.T)
    grad_pair = norm_back(grad_zn * ln_in_gain, normed, inverse).astype(jnp.bfloat16)
    return (grad_pair, contract_pairs(normed_b, grad_p))


def body(
    pair,
    cotangent,
    res_mask,
    chain,
    ln_in_gain,
    ln_in_bias,
    w_proj,
    w_gate,
    chain_bias,
    ln_out_gain,
    ln_out_bias,
    w_out,
):
    tile_rows = pair.shape[0]
    tile_cols = pair.shape[1]
    total = tile_rows * lax.axis_size("row")
    row_start = lax.axis_index("row") * tile_rows
    col_start = lax.axis_index("col") * tile_cols
    maskf = res_mask.astype(jnp.float32)
    mask_rows = lax.dynamic_slice_in_dim(maskf, row_start, tile_rows)
    mask_cols = lax.dynamic_slice_in_dim(maskf, col_start, tile_cols)
    pair_mask = mask_rows[:, None, None] * mask_cols[None, :, None]
    chain_rows = lax.dynamic_slice_in_dim(chain, row_start, tile_rows)
    chain_cols = lax.dynamic_slice_in_dim(chain, col_start, tile_cols)
    same = (chain_rows[:, None] == chain_cols[None, :]).astype(jnp.float32)[:, :, None]
    normed_b, normed, inverse, proj = project(pair, ln_in_gain, ln_in_bias, w_proj)
    act_a, act_b = activations(proj, pair_mask)
    b_cols = lax.all_gather(act_b, "row", axis=0, tiled=True)
    piece = b_cols
    mixed = jnp.transpose(
        lax.psum_scatter(
            jnp.einsum("ikh,jkh->jih", act_a, piece, preferred_element_type=jnp.float32).astype(
                jnp.bfloat16
            ),
            "col",
            scatter_dimension=0,
            tiled=True,
        ).astype(jnp.float32),
        (1, 0, 2),
    )
    grad_mixed, grad_logit, term_out, term_gate = gated_output(
        mixed, cotangent, normed_b, same, chain_bias, w_gate, ln_out_gain, ln_out_bias, w_out
    )
    dx_rows = lax.all_gather(grad_mixed, "col", axis=1, tiled=True)
    grad_a = jnp.einsum("ijh,jkh->ikh", dx_rows, b_cols, preferred_element_type=jnp.float32)
    piece = dx_rows
    grad_b = lax.psum_scatter(
        jnp.einsum("ijh,ikh->jkh", piece, act_a, preferred_element_type=jnp.float32).astype(
            jnp.bfloat16
        ),
        "row",
        scatter_dimension=0,
        tiled=True,
    ).astype(jnp.float32)
    grad_pair, term_proj = input_back(
        normed_b,
        normed,
        inverse,
        proj,
        pair_mask,
        grad_a,
        grad_b,
        grad_logit,
        ln_in_gain,
        w_proj,
        w_gate,
    )
    sums = lax.psum((term_proj, term_gate, term_out), ("row", "col"))
    scale = 1.0 / total
    return (grad_pair, sums[0] * scale, sums[1] * scale, sums[2] * scale)


def solution(mesh):
    return jax.shard_map(
        body,
        mesh=mesh,
        in_specs=(
            P("row", "col", None),
            P("row", "col", None),
            P(),
            P(),
            P(),
            P(),
            P(),
            P(),
            P(),
            P(),
            P(),
            P(),
        ),
        out_specs=(P("row", "col", None), P(), P(), P()),
        check_vma=False,
    )
```

profile of v0, /device:TPU:1, one launch (start us, length us, event | category | flops | bytes accessed | tf_op | source)
XLA Modules:
  0.0 634.5 jit_solution(537603368556544840)
XLA Ops:
  11.2 2.0 fusion.42
  13.3 2.0 copy-done.2
  16.7 1.7 copy.32
  18.4 91.4 %all-gather.3.cloned.1.call-done = bf16[512,32,128]{2,1,0:T(8,128)(2,1)} async-done(((bf16[64,32,128]{2,1,0:T(8,128)(2,1)}), bf16[512,32,128]{2,1,0:T(8,128)(2,1)}) %all-gather.3.cloned.1.call-update) | async-done | bytes 4194320 | tf_op jit(solution)/shard_map/all_gather | solution.py:132
  109.8 8.6 %copy.34 = bf16[512,32,128]{0,1,2:T(8,128)(2,1)} copy(bf16[512,32,128]{2,1,0:T(8,128)(2,1)} %all-gather.3.cloned.1.call-done) | data formatting | bytes 8388608 | tf_op jit(solution)/shard_map/all_gather | solution.py:132
  118.4 7.8 %fusion.59 = bf16[128,512,64]{1,2,0:T(8,128)(2,1)} fusion(bf16[512,32,128]{0,1,2:T(8,128)(2,1)} %copy.34, bf16[64,32,128]{0,1,2:T(8,128)(2,1)S(1)} %copy.32), kind=kOutput, calls=%fused_computation.89 | convolution fusion | flops 268435456 | bytes 13107200 | tf_op jit(solution)/shard_map/ikh,jkh->jih/dot_general | solution.py:136
  126.2 13.0 %copy.33 = bf16[128,512,64]{0,1,2:T(8,128)(2,1)} copy(bf16[128,512,64]{1,2,0:T(8,128)(2,1)} %fusion.59) | data formatting | bytes 16777216 | tf_op jit(solution)/shard_map/ikh,jkh->jih/dot_general | solution.py:136
  140.3 1.9 fusion.6
  142.1 101.5 %reduce-scatter.3.cloned.1.call-done = bf16[32,64,128]{2,0,1:T(8,128)(2,1)} async-done(((bf16[512,64,128]{2,0,1:T(8,128)(2,1)}), bf16[32,64,128]{2,0,1:T(8,128)(2,1)}) %reduce-scatter.3.cloned.1.call-update) | async-done | bytes 524304 | tf_op jit(solution)/shard_map/reduce_scatter | solution.py:135
  246.8 2.6 fusion.58
  249.4 1.9 fusion.35
  251.6 80.1 %all-gather.5.cloned.1.call-done = bf16[64,512,128]{2,1,0:T(8,128)(2,1)} async-done(((bf16[64,32,128]{2,1,0:T(8,128)(2,1)}), bf16[64,512,128]{2,1,0:T(8,128)(2,1)}) %all-gather.5.cloned.1.call-update) | async-done | bytes 8388624 | tf_op jit(solution)/shard_map/all_gather | solution.py:148
  331.8 29.2 %copy.35 = bf16[64,512,128]{0,1,2:T(8,128)(2,1)} copy(bf16[64,512,128]{2,1,0:T(8,128)(2,1)} %all-gather.5.cloned.1.call-done) | data formatting | bytes 16777216 | tf_op jit(solution)/shard_map/all_gather | solution.py:148
  360.9 10.5 %fusion.61 = bf16[128,32,512]{2,1,0:T(8,128)(2,1)} fusion(bf16[64,32,128]{0,1,2:T(8,128)(2,1)S(1)} %copy.32, bf16[64,512,128]{0,1,2:T(8,128)(2,1)} %copy.35), kind=kOutput, calls=%fused_computation.91 | convolution fusion | flops 268435456 | bytes 13107200 | tf_op jit(solution)/shard_map/ijh,ikh->jkh/dot_general | solution.py:152
  371.5 9.1 %copy.39 = bf16[128,32,512]{0,1,2:T(8,128)(2,1)} copy(bf16[128,32,512]{2,1,0:T(8,128)(2,1)} %fusion.61) | data formatting | bytes 8388608 | tf_op jit(solution)/shard_map/ijh,ikh->jkh/dot_general | solution.py:152
  387.2 7.4 %fusion.60 = f32[128,32,64]{2,1,0:T(8,128)S(1)} fusion(bf16[512,32,128]{0,1,2:T(8,128)(2,1)S(1)} %copy-done.1, bf16[64,512,128]{0,1,2:T(8,128)(2,1)} %copy.35), kind=kOutput, calls=%fused_computation.90 | convolution fusion | flops 268435456 | bytes 13631488 | tf_op jit(solution)/shard_map/ijh,jkh->ikh/dot_general | solution.py:149
  394.5 2.5 copy.36
  397.1 71.9 %reduce-scatter.5.cloned.1.call-done = bf16[64,32,128]{2,1,0:T(8,128)(2,1)} async-done(((bf16[512,32,128]{2,1,0:T(8,128)(2,1)}), bf16[64,32,128]{2,1,0:T(8,128)(2,1)}) %reduce-scatter.5.cloned.1.call-update) | async-done | bytes 524304 | tf_op jit(solution)/shard_map/reduce_scatter | solution.py:151
  469.0 3.2 multiply_convert_fusion.3
  473.0 1.8 convolution_bitcast_fusion
  474.8 2.5 fusion.57
  477.4 1.9 fusion.18
  479.3 144.0 %all-reduce.3.cloned.1.call-done = (f32[128,512]{1,0:T(8,128)}, f32[128,128]{1,0:T(8,128)}, f32[128,128]{1,0:T(8,128)}) async-done(((f32[128,512]{1,0:T(8,128)}, f32[128,128]{1,0:T(8,128)}, f32[128,128]{1,0:T(8,128)}), (f32[128,512]{1,0:T(8,128)}, f32[128,128]{1,0:T(8,128)}, f32[128,128]{1,0:T(8,128)})) %all-reduce.3.cloned.1.call-update) | async-done | bytes 393232 | tf_op jit(solution)/shard_map/psum | solution.py:172
  623.3 1.7 broadcast_multiply_fusion
  (72 shorter events, 20.2 us)
Async XLA Ops:
  7.2 4.1 copy-start
  7.2 102.6 %all-gather.3.cloned.1.call-start = ((), (), s32[]{:S(2)}) async-start(), calls=%async_computation.2 | async-start | bytes 4718592 | tf_op jit(solution)/shard_map/all_gather | solution.py:132
  13.3 2.0 copy-start.2
  16.6 227.0 %reduce-scatter.3.cloned.1.call-start = ((), (), s32[]{:S(2)}) async-start(), calls=%async_computation.3 | async-start | bytes 8912896 | tf_op jit(solution)/shard_map/reduce_scatter | solution.py:135
  139.2 0.7 copy-start.16
  139.2 1.1 copy-start.4
  139.2 1.1 copy-start.12
  139.2 1.1 copy-start.14
  139.2 1.1 copy-start.15
  139.2 1.0 copy-start.17
  139.2 107.5 %copy-start.7 = (bf16[64,32,128]{2,1,0:T(8,128)(2,1)S(1)}, bf16[64,32,128]{2,1,0:T(8,128)(2,1)}, u32[]{:S(2)}) copy-start(bf16[64,32,128]{2,1,0:T(8,128)(2,1)} %param.13) | copy-start | bytes 1572868
  139.3 107.5 %copy-start.11 = (bf16[128,128]{1,0:T(8,128)(2,1)S(1)}, bf16[128,128]{1,0:T(8,128)(2,1)}, u32[]{:S(2)}) copy-start(bf16[128,128]{1,0:T(8,128)(2,1)} %param.23) | copy-start | bytes 98308
  139.3 107.5 %copy-start.13 = (f32[128]{0:T(128)S(1)}, f32[128]{0:T(128)}, u32[]{:S(2)}) copy-start(f32[128]{0:T(128)} %param.21) | copy-start | bytes 1540
  139.3 192.5 %all-gather.5.cloned.1.call-start = ((), (), s32[]{:S(2)}) async-start(), calls=%async_computation.4 | async-start | bytes 8912896 | tf_op jit(solution)/shard_map/all_gather | solution.py:148
  243.6 5.8 copy-start.3
  251.4 217.6 %reduce-scatter.5.cloned.1.call-start = ((), (), s32[]{:S(2)}) async-start(), calls=%async_computation.5 | async-start | bytes 4718592 | tf_op jit(solution)/shard_map/reduce_scatter | solution.py:151
  380.6 1.2 copy-start.5
  380.6 1.2 copy-start.18
  380.6 242.7 %all-reduce.3.cloned.1.call-start = ((), (), s32[]{:S(2)}) async-start(), calls=%async_computation.6 | async-start | bytes 786432 | tf_op jit(solution)/shard_map/psum | solution.py:172
  382.8 4.4 copy-start.1
  472.2 0.8 copy-start.10
  472.2 2.6 copy-start.8
  472.2 2.6 copy-start.9
  473.0 1.8 copy-start.6
Sparse Core Ops, SparseCore 0:
  16.7 92.9 all-gather.2
  139.4 104.1 reduce-scatter.2
  251.5 80.1 all-gather.4
  380.7 88.1 reduce-scatter.4
  477.5 145.7 all-reduce.2
where the time goes:
time: 636 us; the launch traced here: 634 us
  waiting for transfers between devices  489 us (77%)
  local copies, waits for them, and re-layouts  69.1 us (11%)
  matrix products  41.8 us (7%)
  other arithmetic  20.2 us (3%)
  between operations  14.1 us (2%)
    psum x1, waiting for transfers between devices, body(): sums = lax.psum((term_proj, term_gate, term_out), ('row', 'col'))  144 us
    reduce_scatter x1, waiting for transfers between devices, body(): lax.psum_scatter(jnp.einsum('ikh,jkh->jih', act_a, piece, preferred_eleme...  101 us
    all_gather x1, waiting for transfers between devices, body(): b_cols = lax.all_gather(act_b, 'row', axis=0, tiled=True)  91.4 us
    all_gather x1, waiting for transfers between devices, body(): dx_rows = lax.all_gather(grad_mixed, 'col', axis=1, tiled=True)  80.1 us
    reduce_scatter x1, waiting for transfers between devices, body(): lax.psum_scatter(jnp.einsum('ijh,ikh->jkh', piece, act_a, preferred_eleme...  71.9 us
    all_gather x1, local copies, waits for them, and re-layouts, body(): dx_rows = lax.all_gather(grad_mixed, 'col', axis=1, tiled=True)  29.2 us
    dot_general x1, local copies, waits for them, and re-layouts, body(): jnp.einsum('ikh,jkh->jih', act_a, piece, preferred_element_type=jnp.float32)  13 us
  transfers between devices with their start and end apart: 5, of which 5 were waited for; matrix products, arithmetic and copies ran while one was open for 3% of the time, Pallas kernels for 0%

commit v1 on v0

--- a/solution.py
+++ b/solution.py
@@ -129,7 +129,10 @@
     same = (chain_rows[:, None] == chain_cols[None, :]).astype(jnp.float32)[:, :, None]
     normed_b, normed, inverse, proj = project(pair, ln_in_gain, ln_in_bias, w_proj)
     act_a, act_b = activations(proj, pair_mask)
-    b_cols = lax.all_gather(act_b, "row", axis=0, tiled=True)
+    devices = lax.axis_size("row")
+    blocks = jnp.stack([act_b for _ in range(devices)])
+    blocks = lax.all_to_all(blocks, "row", split_axis=0, concat_axis=0)
+    b_cols = jnp.concatenate(blocks, axis=0)
     piece = b_cols
     mixed = jnp.transpose(
         lax.psum_scatter(

time: 636 us -> 609 us (0.958)
  waiting for transfers between devices: 489 us -> 454 us
    all_gather x1 -> x0, waiting for transfers between devices: 91.4 us -> none  [body(): b_cols = lax.all_gather(act_b, 'row', axis=0, tiled=True)]
    all_to_all x0 -> x1, waiting for transfers between devices: none -> 57.2 us  [body(): blocks = lax.all_to_all(blocks, 'row', split_axis=0, concat_axis=0)]
    reshape x0 -> x1, local copies, waits for them, and re-layouts: none -> 8.59 us  [body(): b_cols = jnp.concatenate(blocks, axis=0)]
    all_gather x1 -> x0, local copies, waits for them, and re-layouts: 8.59 us -> none  [body(): b_cols = lax.all_gather(act_b, 'row', axis=0, tiled=True)]
where the time goes in v1:
time: 609 us; the launch traced here: 607 us
  waiting for transfers between devices  454 us (75%)
  local copies, waits for them, and re-layouts  71.7 us (12%)
  matrix products  41.8 us (7%)
  other arithmetic  19.4 us (3%)
  between operations  14.1 us (2%)
  starting transfers between devices  6.54 us (1%)
    psum x1, waiting for transfers between devices, body(): sums = lax.psum((term_proj, term_gate, term_out), ('row', 'col'))  144 us
    reduce_scatter x1, waiting for transfers between devices, body(): lax.psum_scatter(jnp.einsum('ikh,jkh->jih', act_a, piece, preferred_eleme...  100 us
    all_gather x1, waiting for transfers between devices, body(): dx_rows = lax.all_gather(grad_mixed, 'col', axis=1, tiled=True)  80.3 us
    reduce_scatter x1, waiting for transfers between devices, body(): lax.psum_scatter(jnp.einsum('ijh,ikh->jkh', piece, act_a, preferred_eleme...  71.9 us
    all_to_all x1, waiting for transfers between devices, body(): blocks = lax.all_to_all(blocks, 'row', split_axis=0, concat_axis=0)  57.2 us
    all_gather x1, local copies, waits for them, and re-layouts, body(): dx_rows = lax.all_gather(grad_mixed, 'col', axis=1, tiled=True)  29.1 us
    dot_general x1, local copies, waits for them, and re-layouts, body(): jnp.einsum('ikh,jkh->jih', act_a, piece, preferred_element_type=jnp.float32)  13 us
  transfers between devices with their start and end apart: 5, of which 5 were waited for; matrix products, arithmetic and copies ran while one was open for 3% of the time, Pallas kernels for 0%

profile of v1, /device:TPU:1, one launch (start us, length us, event | category | flops | bytes accessed | tf_op | source)
XLA Modules:
  0.0 607.3 jit_solution(6065019327762495673)
XLA Ops:
  11.2 2.0 fusion.42
  13.2 2.0 copy-done.2
  15.8 2.7 stack.2
  18.5 6.2 %all-to-all-start = ((bf16[8,64,32,128]{3,2,1,0:T(8,128)(2,1)}), bf16[8,64,32,128]{3,2,1,0:T(8,128)(2,1)}, u32[]{:S(2)}, u32[]{:S(2)}) async-start(bf16[8,64,32,128]{3,2,1,0:T(8,128)(2,1)} %stack.2), calls=%async_computation | async-start | bytes 8388608 | tf_op jit(solution)/shard_map/all_to_all | solution.py:134
  26.5 57.2 %all-to-all-done = bf16[8,64,32,128]{3,2,1,0:T(8,128)(2,1)} async-done(((bf16[8,64,32,128]{3,2,1,0:T(8,128)(2,1)}), bf16[8,64,32,128]{3,2,1,0:T(8,128)(2,1)}, u32[]{:S(2)}, u32[]{:S(2)}) %all-to-all-start) | async-done | bytes 4194336 | tf_op jit(solution)/shard_map/all_to_all | solution.py:134
  83.6 8.6 %copy.33 = bf16[512,32,128]{0,1,2:T(8,128)(2,1)} copy(bf16[512,32,128]{2,1,0:T(8,128)(2,1)} %bitcast.1) | data formatting | bytes 8388608 | tf_op jit(solution)/shard_map/reshape | solution.py:135
  92.2 7.8 %fusion.59 = bf16[128,512,64]{1,2,0:T(8,128)(2,1)} fusion(bf16[512,32,128]{0,1,2:T(8,128)(2,1)} %copy.33, bf16[64,32,128]{0,1,2:T(8,128)(2,1)S(1)} %copy.31), kind=kOutput, calls=%fused_computation.89 | convolution fusion | flops 268435456 | bytes 13107200 | tf_op jit(solution)/shard_map/ikh,jkh->jih/dot_general | solution.py:139
  100.0 13.0 %copy.32 = bf16[128,512,64]{0,1,2:T(8,128)(2,1)} copy(bf16[128,512,64]{1,2,0:T(8,128)(2,1)} %fusion.59) | data formatting | bytes 16777216 | tf_op jit(solution)/shard_map/ikh,jkh->jih/dot_general | solution.py:139
  114.1 1.9 fusion.6
  115.9 100.3 %reduce-scatter.3.cloned.1.call-done = bf16[32,64,128]{2,0,1:T(8,128)(2,1)} async-done(((bf16[512,64,128]{2,0,1:T(8,128)(2,1)}), bf16[32,64,128]{2,0,1:T(8,128)(2,1)}) %reduce-scatter.3.cloned.1.call-update) | async-done | bytes 524304 | tf_op jit(solution)/shard_map/reduce_scatter | solution.py:138
  219.5 2.6 fusion.58
  222.1 1.9 fusion.35
  224.3 80.3 %all-gather.2.cloned.1.call-done = bf16[64,512,128]{2,1,0:T(8,128)(2,1)} async-done(((bf16[64,32,128]{2,1,0:T(8,128)(2,1)}), bf16[64,512,128]{2,1,0:T(8,128)(2,1)}) %all-gather.2.cloned.1.call-update) | async-done | bytes 8388624 | tf_op jit(solution)/shard_map/all_gather | solution.py:151
  304.5 29.1 %copy.34 = bf16[64,512,128]{0,1,2:T(8,128)(2,1)} copy(bf16[64,512,128]{2,1,0:T(8,128)(2,1)} %all-gather.2.cloned.1.call-done) | data formatting | bytes 16777216 | tf_op jit(solution)/shard_map/all_gather | solution.py:151
  333.7 10.5 %fusion.61 = bf16[128,32,512]{2,1,0:T(8,128)(2,1)} fusion(bf16[64,32,128]{0,1,2:T(8,128)(2,1)S(1)} %copy.31, bf16[64,512,128]{0,1,2:T(8,128)(2,1)} %copy.34), kind=kOutput, calls=%fused_computation.91 | convolution fusion | flops 268435456 | bytes 13107200 | tf_op jit(solution)/shard_map/ijh,ikh->jkh/dot_general | solution.py:155
  344.2 9.1 %copy.38 = bf16[128,32,512]{0,1,2:T(8,128)(2,1)} copy(bf16[128,32,512]{2,1,0:T(8,128)(2,1)} %fusion.61) | data formatting | bytes 8388608 | tf_op jit(solution)/shard_map/ijh,ikh->jkh/dot_general | solution.py:155
  359.9 7.4 %fusion.60 = f32[128,32,64]{2,1,0:T(8,128)S(1)} fusion(bf16[512,32,128]{0,1,2:T(8,128)(2,1)S(1)} %copy-done.1, bf16[64,512,128]{0,1,2:T(8,128)(2,1)} %copy.34), kind=kOutput, calls=%fused_computation.90 | convolution fusion | flops 268435456 | bytes 13631488 | tf_op jit(solution)/shard_map/ijh,jkh->ikh/dot_general | solution.py:152
  367.3 2.5 copy.35
  369.8 71.9 %reduce-scatter.5.cloned.1.call-done = bf16[64,32,128]{2,1,0:T(8,128)(2,1)} async-done(((bf16[512,32,128]{2,1,0:T(8,128)(2,1)}), bf16[64,32,128]{2,1,0:T(8,128)(2,1)}) %reduce-scatter.5.cloned.1.call-update) | async-done | bytes 524304 | tf_op jit(solution)/shard_map/reduce_scatter | solution.py:154
  441.7 3.2 multiply_convert_fusion.3
  445.7 1.8 convolution_bitcast_fusion
  447.5 2.5 fusion.57
  450.1 1.9 fusion.18
  452.0 144.1 %all-reduce.3.cloned.1.call-done = (f32[128,512]{1,0:T(8,128)}, f32[128,128]{1,0:T(8,128)}, f32[128,128]{1,0:T(8,128)}) async-done(((f32[128,512]{1,0:T(8,128)}, f32[128,128]{1,0:T(8,128)}, f32[128,128]{1,0:T(8,128)}), (f32[128,512]{1,0:T(8,128)}, f32[128,128]{1,0:T(8,128)}, f32[128,128]{1,0:T(8,128)})) %all-reduce.3.cloned.1.call-update) | async-done | bytes 393232 | tf_op jit(solution)/shard_map/psum | solution.py:175
  (72 shorter events, 22.7 us)
Async XLA Ops:
  7.2 4.1 copy-start
  13.2 2.0 copy-start.2
  18.5 65.1 %all-to-all-start = ((bf16[8,64,32,128]{3,2,1,0:T(8,128)(2,1)}), bf16[8,64,32,128]{3,2,1,0:T(8,128)(2,1)}, u32[]{:S(2)}, u32[]{:S(2)}) async-start(bf16[8,64,32,128]{3,2,1,0:T(8,128)(2,1)} %stack.2), calls=%async_computation | async-start | bytes 8388608 | tf_op jit(solution)/shard_map/all_to_all | solution.py:134
  24.7 191.6 %reduce-scatter.3.cloned.1.call-start = ((), (), s32[]{:S(2)}) async-start(), calls=%async_computation.3 | async-start | bytes 8912896 | tf_op jit(solution)/shard_map/reduce_scatter | solution.py:138
  113.0 0.7 copy-start.16
  113.0 1.1 copy-start.4
  113.0 1.1 copy-start.12
  113.0 1.1 copy-start.14
  113.0 1.1 copy-start.15
  113.0 1.0 copy-start.17
  113.1 106.4 %copy-start.7 = (bf16[64,32,128]{2,1,0:T(8,128)(2,1)S(1)}, bf16[64,32,128]{2,1,0:T(8,128)(2,1)}, u32[]{:S(2)}) copy-start(bf16[64,32,128]{2,1,0:T(8,128)(2,1)} %param.13) | copy-start | bytes 1572868
  113.1 106.4 %copy-start.11 = (bf16[128,128]{1,0:T(8,128)(2,1)S(1)}, bf16[128,128]{1,0:T(8,128)(2,1)}, u32[]{:S(2)}) copy-start(bf16[128,128]{1,0:T(8,128)(2,1)} %param.23) | copy-start | bytes 98308
  113.1 106.4 %copy-start.13 = (f32[128]{0:T(128)S(1)}, f32[128]{0:T(128)}, u32[]{:S(2)}) copy-start(f32[128]{0:T(128)} %param.21) | copy-start | bytes 1540
  113.1 191.4 %all-gather.2.cloned.1.call-start = ((), (), s32[]{:S(2)}) async-start(), calls=%async_computation.4 | async-start | bytes 8912896 | tf_op jit(solution)/shard_map/all_gather | solution.py:151
  216.3 5.8 copy-start.3
  224.0 217.7 %reduce-scatter.5.cloned.1.call-start = ((), (), s32[]{:S(2)}) async-start(), calls=%async_computation.5 | async-start | bytes 4718592 | tf_op jit(solution)/shard_map/reduce_scatter | solution.py:154
  353.3 1.2 copy-start.5
  353.3 1.2 copy-start.18
  353.4 242.8 %all-reduce.3.cloned.1.call-start = ((), (), s32[]{:S(2)}) async-start(), calls=%async_computation.6 | async-start | bytes 786432 | tf_op jit(solution)/shard_map/psum | solution.py:175
  355.5 4.4 copy-start.1
  444.9 0.8 copy-start.10
  444.9 2.6 copy-start.8
  444.9 2.6 copy-start.9
  445.7 1.8 copy-start.6
Sparse Core Ops, SparseCore 0:
  113.2 103.0 reduce-scatter.2
  224.2 80.3 all-gather.1
  353.5 88.1 reduce-scatter.4
  450.2 145.8 all-reduce.2
